TPU v7x, 128 devices: a whole 4x4x4 slice. The times are simulated.
128 devices in a mesh: prompt: 4 (over x), dp: 4 (over y), mp: 8 (over z, core).
Axes of the slice: x: 4, y: 4, z: 4, core: 2. Of those that a mesh axis runs over, the one named last changes fastest.
Arguments:
- prompts: bfloat16 [8, 100, 4096], P('prompt'), may hold values from -6 to 6
- target_embed: bfloat16 [4, 512, 4096], P('dp'), may hold values from -6 to 6
- labels: int32 [4, 512], P('dp'), may hold values from 0 to 16383
- lengths: int32 [4], P('dp'), may hold values from 128 to 512
- attn_gain: float32 [4096], replicated, may hold values from 0.5 to 1.5
- w_qkv: bfloat16 [3, 4096, 2048], P(None, None, 'mp'), may hold values from -4 to 4
- w_out: bfloat16 [2048, 4096], P('mp'), may hold values from -0.5 to 0.5
- final_gain: float32 [4096], replicated, may hold values from 0.5 to 1.5
- w_vocab: bfloat16 [4096, 16384], P(None, ('dp', 'mp')), may hold values from -3 to 3
Outputs:
- token_loss: float32 [8, 4, 512], P('prompt', 'dp')
- prompt_loss: float32 [8], replicated
Inputs may be any that keep to these rules, and one draw needn't show every extreme that they name: `lengths`: positions from a sequence's length on are padding.
All inputs are finite; a program needn't handle non-finite values.
Results may differ from a plain program's by a relative error of at most 0.006.
Values may be sent and summed in bfloat16 or wider, within the bound.
No kernel may reach another device: no remote copies, remote signals or barrier semaphores. Data moves between devices by JAX's collectives and lax.ppermute only.
A program may use at most 128 MiB of HBM per device.

v0:
```python
import math
import jax
import jax.numpy as jnp
from jax import lax
from jax.sharding import Mesh
from jax.sharding import PartitionSpec as P

HD = 128
MP = ("mp_0", "mp_1")
DP_MP = ("dp", "mp_0", "mp_1")
EPSILON = 1e-05
BASE_THETA = 10000.0


def collected_together(value, axis):
    leaves = jax.tree.leaves(value)
    order = sorted(range(len(leaves)), key=lambda k: -leaves[k].size)
    width = (1, *leaves[order[0]].shape)[-1]
    lines = [
        jnp.pad(leaves[k].reshape(-1), (0, -leaves[k].size % width)).reshape(-1, width)
        for k in order
    ]
    both, at, found = (lax.all_gather(jnp.concatenate(lines), axis), 0, {})
    for k, line in zip(order, lines):
        slab = both[:, at : at + len(line)].reshape(len(both), -1)
        found[k] = slab[:, : leaves[k].size].reshape(-1, *leaves[k].shape)
        at += len(line)
    numbers = iter(range(len(leaves)))
    return jax.tree.map(lambda _: found[next(numbers)], value)


def merged_by_axis(value, axes, combine):
    for axis in axes:
        pieces = collected_together(
            jax.tree.map(
                lambda part, kind: part.astype(kind),
                value,
                jax.tree.map(lambda a: jnp.bfloat16 if a.dtype == jnp.float32 else a.dtype, value),
            ),
            axis,
        )
        widened = [
            jax.tree.map(lambda part, own: part[k].astype(own.dtype), pieces, value)
            for k in range(lax.axis_size(axis))
        ]
        value = widened[0]
        for other in widened[1:]:
            value = combine(value, other)
    return value


def sent_to_all(value, axis):
    copies = jnp.broadcast_to(value, (lax.axis_size(axis), *value.shape))
    return lax.all_to_all(copies, axis, split_axis=0, concat_axis=0, tiled=True)


def of_everyone(value, axis):
    everything = sent_to_all(value, axis)
    return jnp.sum(everything, axis=0)


def rms_scaled(values, gain_vec):
    widened = values.astype(jnp.float32)
    return (
        widened
        * lax.rsqrt(jnp.mean(widened * widened, axis=-1, keepdims=True) + EPSILON)
        * gain_vec
    )


def rotate(values, offset, head_dim):
    number_rows = values.shape[-2]
    full_width = values.shape[-1]
    per_head = values.reshape(values.shape[:-1] + (full_width // head_dim, head_dim))
    half_dim = head_dim // 2
    positions = (offset + jnp.arange(number_rows, dtype=jnp.int32)).astype(jnp.float32)
    indices_f = jnp.arange(half_dim, dtype=jnp.int32).astype(jnp.float32)
    frequency = jnp.exp(indices_f * (-2.0 * math.log(BASE_THETA) / head_dim))
    angles = positions[:, None] * frequency[None, :]
    cosine = jnp.cos(angles)[:, None, :]
    sine_part = jnp.sin(angles)[:, None, :]
    first_half = per_head[..., :half_dim]
    second_half = per_head[..., half_dim:]
    turned = jnp.concatenate(
        [
            first_half * cosine - second_half * sine_part,
            second_half * cosine + first_half * sine_part,
        ],
        axis=-1,
    )
    return turned.reshape(values.shape)


def project(normed, weights, offset, rotated_count):
    lead_shape = normed.shape[:-1]
    flat_rows = normed.reshape(-1, normed.shape[-1])
    stacked = jnp.einsum("nd,cde->cne", flat_rows, weights, preferred_element_type=jnp.float32)
    stacked = stacked.reshape((weights.shape[0],) + lead_shape + (weights.shape[2],))
    results = []
    for index_w in range(weights.shape[0]):
        product = stacked[index_w]
        if index_w < rotated_count:
            product = rotate(product, offset, HD)
        results.append(product.astype(jnp.bfloat16))
    return tuple(results)


def attend(prompt_keys, prompt_vals, target_q, target_k, target_v):
    seq_count = target_q.shape[0]
    target_len = target_q.shape[1]
    prompt_len = prompt_keys.shape[0]
    heads_here = target_q.shape[2] // HD
    keys_all = jnp.concatenate([prompt_keys[None], target_k], axis=1)
    vals_all = jnp.concatenate([prompt_vals[None], target_v], axis=1)
    query_h = target_q.reshape(seq_count, target_len, heads_here, HD)
    key_h = keys_all.reshape(seq_count, prompt_len + target_len, heads_here, HD)
    val_h = vals_all.reshape(seq_count, prompt_len + target_len, heads_here, HD)
    scores = jnp.einsum(
        "bqhe,bkhe->bhqk", query_h, key_h, preferred_element_type=jnp.float32
    ) * HD ** (-0.5)
    key_index = jnp.arange(prompt_len + target_len, dtype=jnp.int32)
    query_pos = prompt_len + jnp.arange(target_len, dtype=jnp.int32)
    allowed = key_index[None, :] <= query_pos[:, None]
    scores = jnp.where(allowed[None, None], scores, -1e30)
    top_val = jnp.max(scores, axis=-1, keepdims=True)
    expo = jnp.exp(scores - top_val)
    probs = (expo / jnp.sum(expo, axis=-1, keepdims=True)).astype(jnp.bfloat16)
    context = jnp.einsum("bhqk,bkhe->bqhe", probs, val_h, preferred_element_type=jnp.float32)
    return context.astype(jnp.bfloat16).reshape(seq_count, target_len, heads_here * HD)


def block_stats(normed_rows, label_ids, columns, column_ids):
    logits = jnp.dot(normed_rows, columns, preferred_element_type=jnp.float32)
    top_val = jnp.max(logits, axis=1)
    sum_exp = jnp.sum(jnp.exp(logits - top_val[:, None]), axis=1)
    picked = jnp.sum(jnp.where(column_ids[None, :] == label_ids[:, None], logits, 0.0), axis=1)
    return (top_val, sum_exp, picked)


def combine_stats(earlier, later):
    top_val = jnp.maximum(earlier[0], later[0])
    sum_exp = earlier[1] * jnp.exp(earlier[0] - top_val) + later[1] * jnp.exp(later[0] - top_val)
    return (top_val, sum_exp, earlier[2] + later[2])


def shards(prompts, target_embed, labels, lengths, attn_gain, w_qkv, w_out, final_gain, w_vocab):
    n_prompt = lax.axis_size("prompt")
    n_model = lax.axis_size(MP)
    prompts_here = prompts.shape[0]
    prompt_len = prompts.shape[1]
    seq_count = target_embed.shape[0]
    target_len = target_embed.shape[1]
    model_width = target_embed.shape[2]
    normed_target = rms_scaled(target_embed, attn_gain).astype(jnp.bfloat16)
    target_q, target_k, target_v = project(normed_target, w_qkv, prompt_len, 2)
    normed_prompts = rms_scaled(prompts, attn_gain).astype(jnp.bfloat16)
    prompt_k, prompt_v = project(normed_prompts, w_qkv[1:], 0, 1)

    def one_prompt(pair):
        return attend(pair[0], pair[1], target_q, target_k, target_v)

    contexts = lax.map(one_prompt, (prompt_k, prompt_v))
    ctx_rows = contexts.reshape(-1, contexts.shape[-1])
    total_rows = ctx_rows.shape[0]
    keep_rows = total_rows // n_model
    row_context = lax.all_to_all(ctx_rows, MP, split_axis=0, concat_axis=1, tiled=True)
    full_out = lax.all_gather(w_out, MP, axis=0, tiled=True)
    group_width = w_out.shape[0]
    grouped = jnp.einsum(
        "rgk,gkd->rgd",
        row_context.reshape(keep_rows, n_model, group_width),
        full_out.reshape(n_model, group_width, model_width),
        preferred_element_type=jnp.float32,
    )
    attn_part = jnp.sum(grouped.astype(jnp.bfloat16).astype(jnp.float32), axis=1)
    my_start = lax.axis_index(MP) * keep_rows
    embed_rows = jnp.tile(target_embed.reshape(-1, model_width), (prompts_here, 1))
    residual = lax.dynamic_slice_in_dim(embed_rows, my_start, keep_rows, 0).astype(jnp.float32)
    label_rows = lax.dynamic_slice_in_dim(
        jnp.tile(labels.reshape(-1), prompts_here), my_start, keep_rows, 0
    )
    hidden = residual + attn_part
    normed_out = rms_scaled(hidden, final_gain).astype(jnp.bfloat16)
    vocab_cols = w_vocab.shape[1]
    every_rows, every_labels = (
        lax.all_gather(normed_out, DP_MP, axis=0, tiled=True),
        lax.all_gather(label_rows, DP_MP, axis=0, tiled=True),
    )
    block_index = lax.axis_index("dp") * n_model + lax.axis_index(MP)
    column_ids = block_index * vocab_cols + jnp.arange(vocab_cols, dtype=jnp.int32)
    local_stats = block_stats(every_rows, every_labels, w_vocab, column_ids)
    merged = merged_by_axis(local_stats, DP_MP, combine_stats)
    group_start = lax.axis_index("dp") * total_rows
    merged = tuple(
        (lax.dynamic_slice_in_dim(member, group_start, total_rows, 0) for member in merged)
    )
    losses = (merged[0] + jnp.log(merged[1]) - merged[2]).reshape(
        prompts_here, seq_count, target_len
    )
    valid = jnp.arange(target_len, dtype=jnp.int32)[None, :] < lengths[:, None]
    token_loss = jnp.where(valid[None], losses, 0.0)
    prompt_sums = jnp.sum(token_loss, axis=(1, 2))
    all_prompts = prompts_here * n_prompt
    slot_ids = lax.axis_index("prompt") * prompts_here + jnp.arange(prompts_here, dtype=jnp.int32)
    placed = jnp.sum(
        jnp.where(
            jnp.arange(all_prompts, dtype=jnp.int32)[:, None] == slot_ids[None, :],
            prompt_sums[None, :],
            0.0,
        ),
        axis=1,
    )
    valid_here = jnp.sum(lengths).astype(jnp.float32)
    totals, counted = (
        of_everyone(placed, ("prompt", "dp")),
        of_everyone(valid_here, ("prompt", "dp")),
    )
    prompt_loss = totals * float(n_prompt) / counted
    return (token_loss, prompt_loss)


def solution(mesh):
    finer = Mesh(
        mesh.devices.reshape(mesh.shape["prompt"], mesh.shape["dp"], 4, 2),
        ("prompt", "dp", "mp_0", "mp_1"),
    )
    return jax.shard_map(
        shards,
        mesh=finer,
        in_specs=(
            P("prompt", None, None),
            P("dp", None, None),
            P("dp", None),
            P("dp"),
            P(),
            P(None, None, MP),
            P(MP, None),
            P(),
            P(None, DP_MP),
        ),
        out_specs=(P("prompt", "dp", None), P()),
        check_vma=False,
    )
```

profile of v0, /device:TPU:0, one launch (start us, length us, event | category | flops | bytes accessed | tf_op | source)
XLA Modules:
  0.0 313.7 jit_solution(16696660986336960218)
XLA Ops:
  7.9 3.2 %fusion.36 = f32[2,100]{0,1:T(8,128)S(1)} fusion(bf16[2,100,4096]{2,0,1:T(2,128)(2,1)} %param.11), kind=kLoop, calls=%fused_computation.40 | loop fusion | flops 2457400 | bytes 1639200 | tf_op jit(solution)/shard_map/reduce_sum | solution.py:66
  11.2 2.4 fusion.38
  13.6 1.0 copy.72
  14.9 3.2 %fusion.42 = f32[2,200,256]{2,1,0:T(8,128)S(1)} fusion(bf16[200,4096,1]{1,0,2:T(8,128)(2,1)S(1)} %reshape.1004, bf16[3,4096,256]{2,1,0:T(8,128)(2,1)} %param.16), kind=kOutput, calls=%fused_computation.47 | convolution fusion | flops 838860800 | bytes 6242304 | tf_op jit(solution)/shard_map/nd,cde->cne/dot_general | solution.py:97
  18.2 3.2 %fusion.26 = f32[512]{0:T(512)S(1)} fusion(bf16[1,512,4096]{2,1,0:T(8,128)(2,1)} %param.12), kind=kLoop, calls=%fused_computation.27 | loop fusion | flops 6290944 | bytes 4196352 | tf_op jit(solution)/shard_map/reduce_sum | solution.py:66
  21.5 0.7 copy-done.1
  22.2 6.4 %fusion.39 = f32[3,512,256]{1,2,0:T(8,128)S(1)} fusion(bf16[3,4096,256]{2,1,0:T(8,128)(2,1)} %param.16, bf16[1,512,4096]{2,1,0:T(8,128)(2,1)S(1)} %copy-done.1, f32[4096]{0:T(1024)S(1)} %copy-done.7, f32[512]{0:T(512)S(1)} %add_rsqrt_fusion.1), kind=kOutput, calls=%fused_computation.46 | convolution fusion | flops 3229614080 | bytes 12077056 | tf_op jit(solution)/shard_map/nd,cde->cne/dot_general | solution.py:97
  31.1 8.7 %while.11 = (s32[]{:T(128)}, bf16[2,1,512,256]{3,2,0,1:T(8,128)(2,1)}, bf16[2,100,256]{2,1,0:T(8,128)(2,1)S(1)}, bf16[1,512,256]{1,2,0:T(8,128)(2,1)S(1)}, bf16[...) while((s32[]{:T(128)}, ...), condition=%wide.wide.region_5.6_spmd, body=%wide.wide.region_2.5_spmd.sunk | while | flops 488637120 | bytes 5288549 | solution.py:162
  31.8 1.2 fusion.133
  33.0 1.6 fusion.134
  34.7 0.7 constant_dynamic-update-slice_fusion.3
  36.1 1.2 fusion.133
  37.3 1.6 fusion.134
  39.0 0.7 constant_dynamic-update-slice_fusion.3
  39.7 5.8 %all-to-all-start = ((bf16[8,128,256]{2,1,0:T(8,128)(2,1)}), bf16[8,128,256]{2,1,0:T(8,128)(2,1)S(1)}, u32[]{:S(2)}, u32[]{:S(2)}) async-start(bf16[8,128,256]{2,1,0:T(8,128)(2,1)} %bitcast.18), calls=%async_computation | async-start | bytes 1048576 | tf_op jit(solution)/shard_map/all_to_all | solution.py:166
  45.6 16.2 %all-to-all-done = bf16[8,128,256]{2,1,0:T(8,128)(2,1)S(1)} async-done(((bf16[8,128,256]{2,1,0:T(8,128)(2,1)}), bf16[8,128,256]{2,1,0:T(8,128)(2,1)S(1)}, u32[]{:S(2)}, u32[]{:S(2)}) %all-to-all-start) | async-done | bytes 524320 | tf_op jit(solution)/shard_map/all_to_all | solution.py:166
  61.8 41.2 %all-gather.10.cloned.1.call-done = bf16[2048,4096]{1,0:T(8,128)(2,1)} async-done(((bf16[256,4096]{1,0:T(8,128)(2,1)}), bf16[2048,4096]{1,0:T(8,128)(2,1)}) %all-gather.10.cloned.1.call-update) | async-done | bytes 16777232 | tf_op jit(solution)/shard_map/all_gather | solution.py:167
  103.0 8.6 %convert_reduce_fusion = f32[128,4096]{1,0:T(8,128)S(1)} fusion(bf16[8,256,4096]{2,1,0:T(8,128)(2,1)} %bitcast.276, bf16[8,128,256]{2,1,0:T(8,128)(2,1)} %copy-done.4), kind=kOutput, calls=%fused_computation.24 | convolution fusion | flops 2159542272 | bytes 19398656 | tf_op jit(solution)/shard_map/rgk,gkd->rgd/dot_general | solution.py:169
  111.7 4.3 %tile.21 = bf16[2,512,4096]{2,1,0:T(8,128)(2,1)} broadcast(bf16[512,4096]{1,0:T(8,128)(2,1)S(1)} %bitcast.275), dimensions={1,2} | broadcast | bytes 12582912 | tf_op jit(solution)/shard_map/tile | solution.py:177
  116.0 1.6 multiply_reduce_fusion
  117.6 2.6 multiply_convert_fusion
  121.5 6.8 %all-to-all-start.2 = ((f32[16,1,1]{2,1,0:T(1,128)}), f32[16,1,1]{2,1,0:T(1,128)S(1)}, u32[]{:S(2)}, u32[]{:S(2)}) async-start(f32[16,1,1]{2,1,0:T(1,128)} %broadcast_in_dim.64), calls=%async_computation.2 | async-start | bytes 16384 | tf_op jit(solution)/shard_map/all_to_all | solution.py:54
  128.4 21.5 %all-gather.3 = s32[32,1,128]{2,1,0:T(1,128)S(1)} all-gather(s32[1,1,128]{2,1,0:T(1,128)S(1)} %dynamic-slice_bitcast_fusion), channel_id=1, replica_groups=mesh['prompt'=4,'dp'=4,'mp_0'=4,'mp_1'=2] {'dp','mp_0','mp_1'}, dimensions={0}, use_global_device_ids=true | all-gather | bytes 16896 | tf_op jit(solution)/shard_map/all_gather | solution.py:187
  149.9 84.9 %all-gather.12.cloned.1.call-done = bf16[4096,4096]{1,0:T(8,128)(2,1)} async-done(((bf16[128,4096]{1,0:T(8,128)(2,1)}), bf16[4096,4096]{1,0:T(8,128)(2,1)}) %all-gather.12.cloned.1.call-update) | async-done | bytes 33554448 | tf_op jit(solution)/shard_map/all_gather | solution.py:186
  234.8 24.1 %fusion.105 = (f32[4096]{0:T(1024)S(1)}, f32[4096,512]{0,1:T(8,128)}) fusion(bf16[4096,4096]{1,0:T(8,128)(2,1)} %all-gather.12.cloned.1.call-done, bf16[4096,512]{1,0:T(8,128)(2,1)} %param.19), kind=kOutput, calls=%fused_computation.174 | convolution fusion | flops 17181962240 | bytes 46153728 | tf_op jit(solution)/shard_map/dot_general | solution.py:133
  258.9 4.6 %exponential_reduce_fusion = (bf16[4096]{0:T(1024)(128)(2,1)S(1)}, bf16[4096]{0:T(1024)(128)(2,1)S(1)}) fusion(f32[4096,512]{0,1:T(8,128)} %get-tuple-element.134, f32[4096]{0:T(1024)S(1)} %get-tuple-element.133, s32[4096]{0:T(1024)S(1)} %bitcast.292, s32[512]{0:T(512)S(1)} %iota_add_fusion.1), kind=kLoop, calls=%fused_computation.31 | loop fusion | flops 10477568 | bytes 8439808 | tf_op jit(solution)/shard_map/reduce_sum | solution.py:135
  263.5 12.3 %all-gather.4 = bf16[4,3,4096]{2,1,0:T(4,128)(2,1)S(1)} all-gather(bf16[1,3,4096]{2,1,0:T(4,128)(2,1)S(1)} %maximum_bitcast_fusion), channel_id=2, replica_groups=mesh['prompt'=4,'dp'=4,'mp_0'=4,'mp_1'=2] {'dp'}, dimensions={0}, use_global_device_ids=true | all-gather | bytes 122880 | tf_op jit(solution)/shard_map/all_gather | solution.py:23
  276.2 12.0 %all-gather.5 = bf16[4,3,4096]{2,1,0:T(4,128)(2,1)S(1)} all-gather(bf16[1,3,4096]{2,1,0:T(4,128)(2,1)S(1)} %maximum_bitcast_fusion.1), channel_id=3, replica_groups=mesh['prompt'=4,'dp'=4,'mp_0'=4,'mp_1'=2] {'mp_0'}, dimensions={0}, use_global_device_ids=true | all-gather | bytes 122880 | tf_op jit(solution)/shard_map/all_gather | solution.py:23
  288.5 1.9 all-gather.6
  291.8 6.3 %all-to-all-start.1 = ((f32[16,1,8]{2,1,0:T(1,128)}), f32[16,1,8]{2,1,0:T(1,128)S(1)}, u32[]{:S(2)}, u32[]{:S(2)}) async-start(f32[16,1,8]{2,1,0:T(1,128)} %broadcast_in_dim.59), calls=%async_computation.1 | async-start | bytes 16384 | tf_op jit(solution)/shard_map/all_to_all | solution.py:54
  298.8 6.9 %all-to-all-done.1 = f32[16,1,8]{2,1,0:T(1,128)S(1)} async-done(((f32[16,1,8]{2,1,0:T(1,128)}), f32[16,1,8]{2,1,0:T(1,128)S(1)}, u32[]{:S(2)}, u32[]{:S(2)}) %all-to-all-start.1) | async-done | bytes 544 | tf_op jit(solution)/shard_map/all_to_all | solution.py:54
  305.8 1.1 multiply_divide_fusion
  (87 shorter events, 8.6 us)
Async XLA Ops:
  7.2 121.1 %copy-start = (s32[1,512]{1,0:T(1,128)S(1)}, s32[1,512]{1,0:T(1,128)}, u32[]{:S(2)}) copy-start(s32[1,512]{1,0:T(1,128)} %param.13) | copy-start | bytes 6148
  7.2 4.0 %copy-start.3 = (bf16[2,100,4096]{2,0,1:T(2,128)(2,1)S(1)}, bf16[2,100,4096]{2,0,1:T(2,128)(2,1)}, u32[]{:S(2)}) copy-start(bf16[2,100,4096]{2,0,1:T(2,128)(2,1)} %param.11) | copy-start | bytes 4915204
  7.2 4.0 %copy-start.7 = (f32[4096]{0:T(1024)S(1)}, f32[4096]{0:T(1024)}, u32[]{:S(2)}) copy-start(f32[4096]{0:T(1024)} %param.15) | copy-start | bytes 49156
  7.2 95.8 %all-gather.10.cloned.1.call-start = ((), (), s32[]{:S(2)}) async-start(), calls=%async_computation.3 | async-start | bytes 18874368 | tf_op jit(solution)/shard_map/all_gather | solution.py:167
  18.2 10.5 %copy-start.6 = (f32[2,200,256]{2,1,0:T(8,128)}, f32[2,200,256]{2,1,0:T(8,128)S(1)}, u32[]{:S(2)}) copy-start(f32[2,200,256]{2,1,0:T(8,128)S(1)} %fusion.42) | copy-start | bytes 1228804
  18.2 4.0 %copy-start.1 = (bf16[1,512,4096]{2,1,0:T(8,128)(2,1)S(1)}, bf16[1,512,4096]{2,1,0:T(8,128)(2,1)}, u32[]{:S(2)}) copy-start(bf16[1,512,4096]{2,1,0:T(8,128)(2,1)} %param.12) | copy-start | bytes 12582916
  28.7 1.1 slice-start
  29.7 1.4 copy-start.5
  39.7 22.1 %all-to-all-start = ((bf16[8,128,256]{2,1,0:T(8,128)(2,1)}), bf16[8,128,256]{2,1,0:T(8,128)(2,1)S(1)}, u32[]{:S(2)}, u32[]{:S(2)}) async-start(bf16[8,128,256]{2,1,0:T(8,128)(2,1)} %bitcast.18), calls=%async_computation | async-start | bytes 1048576 | tf_op jit(solution)/shard_map/all_to_all | solution.py:166
  45.5 189.3 %all-gather.12.cloned.1.call-start = ((), (), s32[]{:S(2)}) async-start(), calls=%async_computation.4 | async-start | bytes 34603008 | tf_op jit(solution)/shard_map/all_gather | solution.py:186
  61.8 41.2 %copy-start.4 = (bf16[8,128,256]{2,1,0:T(8,128)(2,1)}, bf16[8,128,256]{2,1,0:T(8,128)(2,1)S(1)}, u32[]{:S(2)}) copy-start(bf16[8,128,256]{2,1,0:T(8,128)(2,1)S(1)} %all-to-all-done) | copy-start | bytes 1572868
  103.0 8.6 %copy-start.2 = (bf16[1,512,4096]{2,1,0:T(8,128)(2,1)S(1)}, bf16[1,512,4096]{2,1,0:T(8,128)(2,1)}, u32[]{:S(2)}) copy-start(bf16[1,512,4096]{2,1,0:T(8,128)(2,1)} %param.12) | copy-start | bytes 12582916
  111.7 5.9 %copy-start.8 = (f32[4096]{0:T(1024)S(1)}, f32[4096]{0:T(1024)}, u32[]{:S(2)}) copy-start(f32[4096]{0:T(1024)} %param.18) | copy-start | bytes 49156
  121.5 169.7 %all-to-all-start.2 = ((f32[16,1,1]{2,1,0:T(1,128)}), f32[16,1,1]{2,1,0:T(1,128)S(1)}, u32[]{:S(2)}, u32[]{:S(2)}) async-start(f32[16,1,1]{2,1,0:T(1,128)} %broadcast_in_dim.64), calls=%async_computation.2 | async-start | bytes 16384 | tf_op jit(solution)/shard_map/all_to_all | solution.py:54
  291.8 13.9 %all-to-all-start.1 = ((f32[16,1,8]{2,1,0:T(1,128)}), f32[16,1,8]{2,1,0:T(1,128)S(1)}, u32[]{:S(2)}, u32[]{:S(2)}) async-start(f32[16,1,8]{2,1,0:T(1,128)} %broadcast_in_dim.59), calls=%async_computation.1 | async-start | bytes 16384 | tf_op jit(solution)/shard_map/all_to_all | solution.py:54
Sparse Core Ops, SparseCore 0:
  9.7 93.2 all-gather.9
  120.4 114.3 all-gather.11
where the time goes:
time: 314 us
  waiting for transfers between devices  150 us (48%)
  matrix products  47.8 us (15%)
  blocking collectives  47.6 us (15%)
  other arithmetic  23.8 us (8%)
  starting transfers between devices  19 us (6%)
  between operations  15.1 us (5%)
  local copies, waits for them, and re-layouts  10.3 us (3%)
    all_gather x1, waiting for transfers between devices, shards(): lax.all_gather(normed_out, DP_MP, axis=0, tiled=True)  84.9 us
    all_gather x1, waiting for transfers between devices, shards(): full_out = lax.all_gather(w_out, MP, axis=0, tiled=True)  41.2 us
    all_gather x3, blocking collectives, collected_together(): both, at, found = (lax.all_gather(jnp.concatenate(lines), axis), 0, {})  26.1 us
    dot_general x1, matrix products, block_stats(): logits = jnp.dot(normed_rows, columns, preferred_element_type=jnp.float32)  24.1 us
    all_gather x1, blocking collectives, shards(): lax.all_gather(label_rows, DP_MP, axis=0, tiled=True)  21.5 us
    all_to_all x1, waiting for transfers between devices, shards(): lax.all_to_all(ctx_rows, MP, split_axis=0, concat_axis=1, tiled=True)  16.2 us
    all_to_all x2, starting transfers between devices, sent_to_all(): return lax.all_to_all(copies, axis, split_axis=0, concat_axis=0, tiled=True)  13.1 us
    dot_general x2, matrix products, project(): jnp.einsum('nd,cde->cne', flat_rows, weights, preferred_element_type=jnp....  9.64 us
  transfers between devices with their start and end apart: 5, of which 4 were waited for; matrix products, arithmetic and copies ran while one was open for 20% of the time, Pallas kernels for 0%

commit v1 on v0

--- a/solution.py
+++ b/solution.py
@@ -164,7 +164,8 @@
     total_rows = ctx_rows.shape[0]
     keep_rows = total_rows // n_model
     row_context = lax.all_to_all(ctx_rows, MP, split_axis=0, concat_axis=1, tiled=True)
-    full_out = lax.all_gather(w_out, MP, axis=0, tiled=True)
+    outgoing = jnp.stack([w_out] * lax.axis_size(MP))
+    full_out = jnp.concatenate(lax.all_to_all(outgoing, MP, 0, 0), axis=0)
     group_width = w_out.shape[0]
     grouped = jnp.einsum(
         "rgk,gkd->rgd",

time: 314 us -> 459 us (1.46)
  waiting for transfers between devices: 150 us -> 275 us
  blocking collectives: 47.6 us -> 63.1 us
  local copies, waits for them, and re-layouts: 10.3 us -> 15 us
    all_to_all x1, waiting for transfers between devices: 16.2 us -> 184 us  [shards(): full_out = jnp.concatenate(lax.all_to_all(outgoing, MP, 0, 0), axis=0)]
    all_gather x1 -> x0, waiting for transfers between devices: 41.2 us -> none  [shards(): full_out = lax.all_gather(w_out, MP, axis=0, tiled=True)]
    all_to_all x0 -> x1, blocking collectives: none -> 15.7 us  [shards(): lax.all_to_all(ctx_rows, MP, split_axis=0, concat_axis=1, tiled=True)]
    another operation x1 -> x2, local copies, waits for them, and re-layouts: 0.07 us -> 6.94 us  [the longest x1 6.87 us: shards(): outgoing = jnp.stack([w_out] * lax.axis_size(MP))]
  transfers between devices with their start and end apart: 5 -> 4, of which waited for: 4 -> 3; matrix products, arithmetic and copies ran while one was open for 20% -> 7% of each run, Pallas kernels for 0% -> 0%
where the time goes in v1:
time: 459 us; the launch traced here: 458 us
  waiting for transfers between devices  275 us (60%)
  blocking collectives  63.1 us (14%)
  matrix products  47.6 us (10%)
  other arithmetic  22.7 us (5%)
  starting transfers between devices  19.4 us (4%)
  between operations  15.1 us (3%)
  local copies, waits for them, and re-layouts  15 us (3%)
    all_to_all x1, waiting for transfers between devices, shards(): full_out = jnp.concatenate(lax.all_to_all(outgoing, MP, 0, 0), axis=0)  184 us
    all_gather x1, waiting for transfers between devices, shards(): lax.all_gather(normed_out, DP_MP, axis=0, tiled=True)  83.9 us
    all_gather x3, blocking collectives, collected_together(): both, at, found = (lax.all_gather(jnp.concatenate(lines), axis), 0, {})  26.1 us
    dot_general x1, matrix products, block_stats(): logits = jnp.dot(normed_rows, columns, preferred_element_type=jnp.float32)  24.1 us
    all_gather x1, blocking collectives, shards(): lax.all_gather(label_rows, DP_MP, axis=0, tiled=True)  21.2 us
    all_to_all x1, blocking collectives, shards(): lax.all_to_all(ctx_rows, MP, split_axis=0, concat_axis=1, tiled=True)  15.7 us
    all_to_all x2, starting transfers between devices, sent_to_all(): return lax.all_to_all(copies, axis, split_axis=0, concat_axis=0, tiled=True)  13.4 us
    dot_general x2, matrix products, project(): jnp.einsum('nd,cde->cne', flat_rows, weights, preferred_element_type=jnp....  9.47 us
  transfers between devices with their start and end apart: 4, of which 3 were waited for; matrix products, arithmetic and copies ran while one was open for 7% of the time, Pallas kernels for 0%

profile of v1, /device:TPU:0, one launch (start us, length us, event | category | flops | bytes accessed | tf_op | source)
XLA Modules:
  0.0 458.2 jit_solution(1393902133105044453)
XLA Ops:
  7.2 3.2 fusion.36
  10.4 3.8 fusion.38
  14.2 1.0 copy.72
  15.5 3.4 fusion.42
  19.0 0.9 fusion.26
  19.9 6.1 %fusion.39 = f32[3,512,256]{1,2,0:T(8,128)S(1)} fusion(bf16[3,4096,256]{2,1,0:T(8,128)(2,1)} %param.16, bf16[1,512,4096]{2,1,0:T(8,128)(2,1)S(1)} %copy-done.1, f32[4096]{0:T(1024)S(1)} %copy-done.5, f32[512]{0:T(512)S(1)} %add_rsqrt_fusion.1), kind=kOutput, calls=%fused_computation.46 | convolution fusion | flops 3229614080 | bytes 12077056 | tf_op jit(solution)/shard_map/nd,cde->cne/dot_general | solution.py:97
  28.4 7.3 %while.11 = (s32[]{:T(128)}, bf16[2,1,512,256]{3,2,0,1:T(8,128)(2,1)S(1)}, bf16[2,100,256]{2,1,0:T(8,128)(2,1)S(1)}, bf16[1,512,256]{1,2,0:T(8,128)(2,1)S(1)}, b...) while((s32[]{:T(128)}, ...), condition=%wide.wide.region_5.6_spmd, body=%wide.wide.region_2.5_spmd.sunk | while | flops 488637120 | bytes 5288041 | solution.py:162
  29.1 1.2 fusion.133
  30.3 1.6 fusion.134
  32.8 1.2 fusion.133
  34.0 1.6 fusion.134
  35.7 15.7 %all_to_all.33 = bf16[8,128,256]{2,1,0:T(8,128)(2,1)} all-to-all(bf16[8,128,256]{2,1,0:T(8,128)(2,1)S(1)} %bitcast.286), channel_id=1, replica_groups=mesh['prompt'=4,'dp'=4,'mp_0'=4,'mp_1'=2] {'mp_0','mp_1'}, dimensions={0} | all-to-all | bytes 1048576 | tf_op jit(solution)/shard_map/all_to_all | solution.py:166
  51.4 6.9 %stack.2 = bf16[8,256,4096]{2,1,0:T(8,128)(2,1)} broadcast(bf16[256,4096]{1,0:T(8,128)(2,1)} %param.17), dimensions={1,2} | broadcast | bytes 18874368 | tf_op jit(solution)/shard_map/stack | solution.py:167
  58.3 5.8 %all-to-all-start.1 = ((bf16[8,256,4096]{2,1,0:T(8,128)(2,1)}), bf16[8,256,4096]{2,1,0:T(8,128)(2,1)}, u32[]{:S(2)}, u32[]{:S(2)}) async-start(bf16[8,256,4096]{2,1,0:T(8,128)(2,1)} %stack.2), calls=%async_computation.1 | async-start | bytes 33554432 | tf_op jit(solution)/shard_map/all_to_all | solution.py:168
  64.3 184.2 %all-to-all-done.1 = bf16[8,256,4096]{2,1,0:T(8,128)(2,1)} async-done(((bf16[8,256,4096]{2,1,0:T(8,128)(2,1)}), bf16[8,256,4096]{2,1,0:T(8,128)(2,1)}, u32[]{:S(2)}, u32[]{:S(2)}) %all-to-all-start.1) | async-done | bytes 16777248 | tf_op jit(solution)/shard_map/all_to_all | solution.py:168
  248.5 8.6 %convert_reduce_fusion = f32[128,4096]{1,0:T(8,128)S(1)} fusion(bf16[8,256,4096]{2,1,0:T(8,128)(2,1)} %all-to-all-done.1, bf16[8,128,256]{2,1,0:T(8,128)(2,1)} %all_to_all.33), kind=kOutput, calls=%fused_computation.24 | convolution fusion | flops 2159542272 | bytes 19398656 | tf_op jit(solution)/shard_map/rgk,gkd->rgd/dot_general | solution.py:170
  257.2 4.3 tile.21
  261.5 1.6 multiply_reduce_fusion
  263.1 2.6 multiply_convert_fusion
  267.0 7.0 %all-to-all-start.3 = ((f32[16,1,1]{2,1,0:T(1,128)}), f32[16,1,1]{2,1,0:T(1,128)S(1)}, u32[]{:S(2)}, u32[]{:S(2)}) async-start(f32[16,1,1]{2,1,0:T(1,128)} %broadcast_in_dim.64), calls=%async_computation.3 | async-start | bytes 16384 | tf_op jit(solution)/shard_map/all_to_all | solution.py:54
  274.1 21.2 %all-gather.3 = s32[32,1,128]{2,1,0:T(1,128)S(1)} all-gather(s32[1,1,128]{2,1,0:T(1,128)S(1)} %dynamic-slice_bitcast_fusion), channel_id=1, replica_groups=mesh['prompt'=4,'dp'=4,'mp_0'=4,'mp_1'=2] {'dp','mp_0','mp_1'}, dimensions={0}, use_global_device_ids=true | all-gather | bytes 16896 | tf_op jit(solution)/shard_map/all_gather | solution.py:188
  295.4 83.9 %all-gather.9.cloned.1.call-done = bf16[4096,4096]{1,0:T(8,128)(2,1)} async-done(((bf16[128,4096]{1,0:T(8,128)(2,1)}), bf16[4096,4096]{1,0:T(8,128)(2,1)}) %all-gather.9.cloned.1.call-update) | async-done | bytes 33554448 | tf_op jit(solution)/shard_map/all_gather | solution.py:187
  379.3 24.1 %fusion.105 = (f32[4096]{0:T(1024)S(1)}, f32[4096,512]{0,1:T(8,128)}) fusion(bf16[4096,4096]{1,0:T(8,128)(2,1)} %all-gather.9.cloned.1.call-done, bf16[4096,512]{1,0:T(8,128)(2,1)} %param.19), kind=kOutput, calls=%fused_computation.174 | convolution fusion | flops 17181962240 | bytes 46153728 | tf_op jit(solution)/shard_map/dot_general | solution.py:133
  403.4 4.6 exponential_reduce_fusion
  408.1 12.3 %all-gather.4 = bf16[4,3,4096]{2,1,0:T(4,128)(2,1)S(1)} all-gather(bf16[1,3,4096]{2,1,0:T(4,128)(2,1)S(1)} %maximum_bitcast_fusion), channel_id=2, replica_groups=mesh['prompt'=4,'dp'=4,'mp_0'=4,'mp_1'=2] {'dp'}, dimensions={0}, use_global_device_ids=true | all-gather | bytes 122880 | tf_op jit(solution)/shard_map/all_gather | solution.py:23
  420.7 12.0 %all-gather.5 = bf16[4,3,4096]{2,1,0:T(4,128)(2,1)S(1)} all-gather(bf16[1,3,4096]{2,1,0:T(4,128)(2,1)S(1)} %maximum_bitcast_fusion.1), channel_id=3, replica_groups=mesh['prompt'=4,'dp'=4,'mp_0'=4,'mp_1'=2] {'mp_0'}, dimensions={0}, use_global_device_ids=true | all-gather | bytes 122880 | tf_op jit(solution)/shard_map/all_gather | solution.py:23
  433.1 1.9 all-gather.6
  435.1 0.6 fusion.100
  436.4 6.3 %all-to-all-start.2 = ((f32[16,1,8]{2,1,0:T(1,128)}), f32[16,1,8]{2,1,0:T(1,128)S(1)}, u32[]{:S(2)}, u32[]{:S(2)}) async-start(f32[16,1,8]{2,1,0:T(1,128)} %broadcast_in_dim.59), calls=%async_computation.2 | async-start | bytes 16384 | tf_op jit(solution)/shard_map/all_to_all | solution.py:54
  442.7 0.6 reduce_sum.112
  443.3 6.9 %all-to-all-done.2 = f32[16,1,8]{2,1,0:T(1,128)S(1)} async-done(((f32[16,1,8]{2,1,0:T(1,128)}), f32[16,1,8]{2,1,0:T(1,128)S(1)}, u32[]{:S(2)}, u32[]{:S(2)}) %all-to-all-start.2) | async-done | bytes 544 | tf_op jit(solution)/shard_map/all_to_all | solution.py:54
  450.3 1.1 multiply_divide_fusion
  (82 shorter events, 7.0 us)
Async XLA Ops:
  7.2 266.9 %copy-start = (s32[1,512]{1,0:T(1,128)S(1)}, s32[1,512]{1,0:T(1,128)}, u32[]{:S(2)}) copy-start(s32[1,512]{1,0:T(1,128)} %param.13) | copy-start | bytes 6148
  15.5 3.5 copy-start.1
  18.9 0.9 copy-start.4
  18.9 1.0 copy-start.5
  26.0 1.4 slice-start
  27.0 1.4 copy-start.3
  58.3 190.3 %all-to-all-start.1 = ((bf16[8,256,4096]{2,1,0:T(8,128)(2,1)}), bf16[8,256,4096]{2,1,0:T(8,128)(2,1)}, u32[]{:S(2)}, u32[]{:S(2)}) async-start(bf16[8,256,4096]{2,1,0:T(8,128)(2,1)} %stack.2), calls=%async_computation.1 | async-start | bytes 33554432 | tf_op jit(solution)/shard_map/all_to_all | solution.py:168
  64.0 315.3 %all-gather.9.cloned.1.call-start = ((), (), s32[]{:S(2)}) async-start(), calls=%async_computation.4 | async-start | bytes 34603008 | tf_op jit(solution)/shard_map/all_gather | solution.py:187
  248.5 8.6 %copy-start.2 = (bf16[1,512,4096]{2,1,0:T(8,128)(2,1)S(1)}, bf16[1,512,4096]{2,1,0:T(8,128)(2,1)}, u32[]{:S(2)}) copy-start(bf16[1,512,4096]{2,1,0:T(8,128)(2,1)} %param.12) | copy-start | bytes 12582916
  257.2 5.9 %copy-start.6 = (f32[4096]{0:T(1024)S(1)}, f32[4096]{0:T(1024)}, u32[]{:S(2)}) copy-start(f32[4096]{0:T(1024)} %param.18) | copy-start | bytes 49156
  267.0 168.8 %all-to-all-start.3 = ((f32[16,1,1]{2,1,0:T(1,128)}), f32[16,1,1]{2,1,0:T(1,128)S(1)}, u32[]{:S(2)}, u32[]{:S(2)}) async-start(f32[16,1,1]{2,1,0:T(1,128)} %broadcast_in_dim.64), calls=%async_computation.3 | async-start | bytes 16384 | tf_op jit(solution)/shard_map/all_to_all | solution.py:54
  436.4 13.9 %all-to-all-start.2 = ((f32[16,1,8]{2,1,0:T(1,128)}), f32[16,1,8]{2,1,0:T(1,128)S(1)}, u32[]{:S(2)}, u32[]{:S(2)}) async-start(f32[16,1,8]{2,1,0:T(1,128)} %broadcast_in_dim.59), calls=%async_computation.2 | async-start | bytes 16384 | tf_op jit(solution)/shard_map/all_to_all | solution.py:54
Sparse Core Ops, SparseCore 0:
  265.9 113.4 all-gather.8
